TPU v7x, 128 devices: a whole 4x4x4 slice. The times are simulated.
128 devices in a mesh: inst: 8 (over z_lo, x), space: 16 (over z_hi, y, core).
Axes of the slice: x: 4, y: 4, z: 4 (z_hi: 2, z_lo: 2; z = z_hi * 2 + z_lo), core: 2. Of those that a mesh axis runs over, the one named last changes fastest.
Arguments:
- field_start: float32 [32, 256, 64, 128], P('inst', 'space'), may hold values from -6 to 6
- source: float32 [32, 256, 64, 128], P('inst', 'space'), may hold values from -6 to 6
- material: int32 [256, 64, 128], P('space'), may hold values from 0 to 7
- face_flags: int32 [32, 3, 256, 64, 128], P('inst', None, 'space'), may hold values from 0 to 1
- disp_table: float32 [8], replicated, may hold values from 0.3 to 3
- perm_table: float32 [8], replicated, may hold values from 0.2 to 2
Outputs:
- residual: float32 [32, 256, 64, 128], P('inst', 'space')
- field: float32 [32, 256, 64, 128], P('inst', 'space')
All inputs are finite; a program needn't handle non-finite values.
Results may differ from a plain program's by a relative error of at most 0.00005.
Values sent between devices are 32-bit elements; how exact they have to be, the bound alone decides.
A program may use at most 128 MiB of HBM per device.

v0:
```python
import jax
import jax.numpy as jnp
from jax import lax
from jax.sharding import PartitionSpec as P

NT = 32
omega_scale = 0.25
decay_rate = 0.3
relax_weight = 0.8


def shifted(shard, axis, by):
    count = lax.axis_size(axis)
    pairs = [(i, i + by) for i in range(count) if 0 <= i + by < count]
    return lax.ppermute(shard, axis, pairs)


def with_halo(block, sides, width):
    for axis, dim in sides:
        count = lax.axis_size(axis)
        forward = [(i, i + 1) for i in range(count - 1)]
        backward = [(target, source) for source, target in forward]
        low = lax.ppermute(
            lax.slice_in_dim(block, block.shape[dim] - width, None, axis=dim), axis, forward
        )
        high = lax.ppermute(lax.slice_in_dim(block, 0, width, axis=dim), axis, backward)
        block = jnp.concatenate([low, block, high], axis=dim)
    return block


def spectral_matrix(first, count):
    rows = first + jnp.arange(count)
    cols = jnp.arange(NT)
    diff = rows[:, None] - cols[None, :]
    angle = jnp.pi * diff.astype(jnp.float32) / NT
    parity = 1.0 - 2.0 * (diff % 2).astype(jnp.float32)
    safe = jnp.where(diff == 0, 1.0, jnp.sin(angle))
    return jnp.where(diff == 0, 0.0, 0.5 * parity * jnp.cos(angle) / safe)


def lookup(material, table):
    total = jnp.zeros(material.shape, jnp.float32)
    for klass in range(table.shape[0]):
        total = total + jnp.where(material == klass, table[klass], 0.0)
    return total


def next_along(field, axis):
    count = field.shape[axis]
    zeros = jnp.zeros_like(lax.slice_in_dim(field, 0, 1, axis=axis))
    return jnp.concatenate([lax.slice_in_dim(field, 1, count, axis=axis), zeros], axis)


def prev_along(field, axis):
    count = field.shape[axis]
    zeros = jnp.zeros_like(lax.slice_in_dim(field, 0, 1, axis=axis))
    return jnp.concatenate([zeros, lax.slice_in_dim(field, 0, count - 1, axis=axis)], axis)


def face_terms(field, up_val, lo_val, kappa, lo_kappa, flow, lo_flow):
    return (
        kappa * (field - up_val)
        + lo_kappa * (field - lo_val)
        + jnp.maximum(flow, 0.0) * field
        + jnp.minimum(flow, 0.0) * up_val
        - jnp.maximum(lo_flow, 0.0) * lo_val
        - jnp.minimum(lo_flow, 0.0) * field
    )


def diag_terms(kappa, lo_kappa, flow, lo_flow):
    return kappa + lo_kappa + jnp.maximum(flow, 0.0) - jnp.minimum(lo_flow, 0.0)


def body(field_start, source, material, face_flags, disp_table, perm_table):
    count = field_start.shape[0]
    first = lax.axis_index("inst") * count
    kappa = lookup(material, disp_table)
    speed = lookup(material, perm_table)
    moments = (first + jnp.arange(count)).astype(jnp.float32)
    tide = 1.0 + 0.5 * jnp.cos(2.0 * jnp.pi * moments / NT)
    velocity = (
        speed[None, None]
        * tide[:, None, None, None, None]
        * (1.0 - 2.0 * face_flags.astype(jnp.float32))
    )
    top_plane = jnp.concatenate([kappa[-1:], velocity[:, 0, -1]], 0)
    below = shifted(top_plane, "space", 1)
    low_kappa_z = jnp.concatenate([below[:1], kappa[:-1]], 0)
    low_flow_z = jnp.concatenate([below[1:, None], velocity[:, 0, :-1]], 1)
    kappa_wide = kappa[None]
    diag = decay_rate + jnp.zeros_like(field_start)
    diag = diag + diag_terms(kappa_wide, low_kappa_z[None], velocity[:, 0], low_flow_z)
    for axis in (1, 2):
        flow = velocity[:, axis]
        diag = diag + diag_terms(
            kappa_wide, prev_along(kappa, axis)[None], flow, prev_along(flow, axis + 1)
        )
    dmat_rows = spectral_matrix(first, count)

    def coupled(field):
        piece = lax.all_gather(field, "inst", axis=0, tiled=True)
        flat = piece.reshape(piece.shape[0], -1)
        product = jnp.dot(
            dmat_rows, flat, precision=lax.Precision.HIGHEST, preferred_element_type=jnp.float32
        )
        return product.reshape(jnp.zeros(field.shape, jnp.float32).shape)

    def residual_of(field):
        padded = with_halo(field, (("space", 1),), 1)
        total = decay_rate * field
        total = total + face_terms(
            field,
            padded[:, 2:],
            padded[:, :-2],
            kappa_wide,
            low_kappa_z[None],
            velocity[:, 0],
            low_flow_z,
        )
        for axis in (1, 2):
            flow = velocity[:, axis]
            total = total + face_terms(
                field,
                next_along(field, axis + 1),
                prev_along(field, axis + 1),
                kappa_wide,
                prev_along(kappa, axis)[None],
                flow,
                prev_along(flow, axis + 1),
            )
        return omega_scale * coupled(field) + total - source

    residual = residual_of(field_start)
    middle = field_start - relax_weight * residual / diag
    second = residual_of(middle)
    field = middle - relax_weight * second / diag
    return (residual, field)


def solution(mesh):
    return jax.shard_map(
        body,
        mesh=mesh,
        in_specs=(
            P("inst", "space", None, None),
            P("inst", "space", None, None),
            P("space", None, None),
            P("inst", None, "space", None, None),
            P(),
            P(),
        ),
        out_specs=(P("inst", "space", None, None), P("inst", "space", None, None)),
        check_vma=False,
    )
```

profile of v0, /device:TPU:1, one launch (start us, length us, event | category | flops | bytes accessed | tf_op | source)
XLA Modules:
  0.0 476.9 jit_solution(4694018413515174211)
XLA Ops:
  9.5 3.3 collective-permute-start
  12.8 3.2 collective-permute-start.2
  16.7 7.8 %select_add_fusion.1 = (f32[16,64,128]{2,1,0:T(8,128)S(1)}, pred[16,64,128]{2,1,0:T(8,128)(4,1)S(1)}, pred[16,64,128]{2,1,0:T(8,128)(4,1)S(1)}, pred[16,64,128]{...) fusion(f32[]{:T(128)} %bitcast.10, f32[]{:T(128)} %bitcast.9, ...), kind=kLoop, calls=%fused_computation.68 | loop fusion | flops 3014656 | bytes 2097184 | tf_op jit(solution)/shard_map/add | solution.py:44
  25.8 6.5 %select_add_fusion = f32[16,64,128]{2,1,0:T(8,128)S(1)} fusion(pred[16,64,128]{2,1,0:T(8,128)(4,1)} %get-tuple-element.18, pred[16,64,128]{2,1,0:T(8,128)(4,1)S(1)} %get-tuple-element.17, pred[16,64,128]{2,1,0:T(8,128)(4,1)S(1)} %get-tuple-element.16, pred[16,64,128]{2,1,0:T(8,128)(4,1)S(1)} %get-tuple-element.15, ...), kind=kLoop, calls=%fused_computation.67 | loop fusion | flops 1966080 | bytes 1572896 | tf_op jit(solution)/shard_map/add | solution.py:44
  32.6 4.0 fusion.6
  36.7 2.3 collective-permute-start.1
  39.0 2.4 slice_bitcast_fusion.1
  41.4 2.4 fusion.81
  43.9 2.9 fusion.82
  48.3 1.9 pad_maximum_fusion.5
  50.1 135.6 %all-gather.3.cloned.1.call-done = f32[32,16,64,128]{3,2,1,0:T(8,128)} async-done(((f32[4,16,64,128]{3,2,1,0:T(8,128)}), f32[32,16,64,128]{3,2,1,0:T(8,128)}) %all-gather.3.cloned.1.call-update) | async-done | bytes 16777232 | tf_op jit(solution)/shard_map/all_gather | solution.py:102
  185.7 15.2 %copy.176 = f32[4,8,1024,128]{3,1,2,0:T(8,128)S(1)} copy(f32[4,8,1024,128]{3,2,1,0:T(8,128)} %bitcast.116) | data formatting | bytes 33554432
  200.9 6.9 %copy.152 = f32[4,8,1024,128]{3,2,1,0:T(8,128)} copy(f32[4,8,1024,128]{3,1,2,0:T(8,128)S(1)} %copy.176) | data formatting | bytes 33554432
  207.8 25.3 %fusion.2 = f32[4,16,64,128]{3,0,2,1:T(4,128)} fusion(f32[16,64,128,32]{2,1,0,3:T(8,128)} %bitcast.109, s32[4]{0:T(128)S(1)} %iota_add_fusion), kind=kOutput, calls=%fused_computation.4 | convolution fusion | flops 201329536 | bytes 18874384 | tf_op jit(solution)/shard_map/dot_general | solution.py:104
  233.2 11.2 %divide_subtract_fusion = (f32[4,16,64,128]{3,2,1,0:T(8,128)}, f32[4,16,64,128]{3,2,1,0:T(8,128)}) fusion(f32[4,16,64,128]{3,2,1,0:T(8,128)S(1)} %copy-done.2, f32[4,16,64,127]{3,2,1,0:T(8,128)S(1)} %bitcast.114, f32[4,16,63,128]{3,2,1,0:T(8,128)S(1)} %bitcast.112, f32[4,3,16,64,128]{4,3,2,0,1:T(8,128)S(1)} %bitcast.105, ...), kind=kLoop, calls=%fused_computation.61 | loop fusion | flops 38273024 | bytes 35241984 | tf_op jit(solution)/shard_map/sub | solution.py:135
  246.7 2.6 collective-permute-start.3
  249.3 2.9 collective-permute-start.4
  252.2 2.4 fusion.77
  254.7 2.9 fusion.78
  257.6 155.4 %all-gather.5.cloned.1.call-done = f32[32,16,64,128]{3,2,1,0:T(8,128)} async-done(((f32[4,16,64,128]{3,2,1,0:T(8,128)}), f32[32,16,64,128]{3,2,1,0:T(8,128)}) %all-gather.5.cloned.1.call-update) | async-done | bytes 16777232 | tf_op jit(solution)/shard_map/all_gather | solution.py:102
  413.0 15.2 %copy.175 = f32[4,8,1024,128]{3,1,2,0:T(8,128)S(1)} copy(f32[4,8,1024,128]{3,2,1,0:T(8,128)} %bitcast.117) | data formatting | bytes 33554432
  428.2 6.9 %copy.154 = f32[4,8,1024,128]{3,2,1,0:T(8,128)} copy(f32[4,8,1024,128]{3,1,2,0:T(8,128)S(1)} %copy.175) | data formatting | bytes 33554432
  435.1 24.9 %fusion = f32[4,16,64,128]{3,0,2,1:T(4,128)} fusion(f32[16,64,128,32]{2,1,0,3:T(8,128)} %bitcast.108, s32[4]{0:T(128)S(1)} %iota_add_fusion), kind=kOutput, calls=%fused_computation.2 | convolution fusion | flops 201329536 | bytes 18874384 | tf_op jit(solution)/shard_map/dot_general | solution.py:104
  460.1 9.8 %fusion.18 = f32[4,16,64,128]{3,2,1,0:T(8,128)} fusion(f32[4,16,64,128]{3,2,1,0:T(8,128)S(1)} %copy-done, f32[4,16,64,128]{3,2,1,0:T(8,128)} %param.7, f32[4,1,64,128]{3,2,1,0:T(8,128)S(1)} %collective-permute-done.4, f32[4,1,64,128]{3,2,1,0:T(8,128)S(1)} %collective-permute-done.3, f32[4,16,64,128]{3,0,2,1:T(4,128)} %fusion, ...), kind=kLoop, calls=%fused_computation.22 | loop fusion | flops 38273024 | bytes 33144832 | tf_op jit(solution)/shard_map/sub | solution.py:137
  (57 shorter events, 8.4 us)
Async XLA Ops:
  7.2 1.6 copy-start.2
  7.2 8.8 %copy-start.10 = (f32[8]{0:T(128)S(1)}, f32[8]{0:T(128)}, u32[]{:S(2)}) copy-start(f32[8]{0:T(128)} %param.10) | copy-start | bytes 100
  7.2 17.9 %copy-start.11 = (f32[8]{0:T(128)S(1)}, f32[8]{0:T(128)}, u32[]{:S(2)}) copy-start(f32[8]{0:T(128)} %param.11) | copy-start | bytes 100
  7.2 178.5 %all-gather.3.cloned.1.call-start = ((), (), s32[]{:S(2)}) async-start(), calls=%async_computation | async-start | bytes 18874368 | tf_op jit(solution)/shard_map/all_gather | solution.py:102
  7.9 405.1 %all-gather.5.cloned.1.call-start = ((), (), s32[]{:S(2)}) async-start(), calls=%async_computation.1 | async-start | bytes 18874368 | tf_op jit(solution)/shard_map/all_gather | solution.py:102
  9.5 223.7 %collective-permute-start = (f32[4,1,64,128]{3,2,1,0:T(8,128)}, f32[4,1,64,128]{3,2,1,0:T(8,128)}, u32[]{:S(2)}, u32[]{:S(2)}) collective-permute-start(f32[4,1,64,128]{3,2,1,0:T(8,128)} %get-tuple-element.27), channel_id=1, source_target_pairs={{1,0},{2,1},{3,2},{4,3},{5,4},{6,5},{7,6},{8,7},{9,8},{10,9},{11,1... | collective-permute-start | bytes 393224 | tf_op jit(solution)/shard_map/ppermute | solution.py:26
  12.8 220.3 %collective-permute-start.2 = (f32[4,1,64,128]{3,2,1,0:T(8,128)}, f32[4,1,64,128]{3,2,1,0:T(8,128)}, u32[]{:S(2)}, u32[]{:S(2)}) collective-permute-start(f32[4,1,64,128]{3,2,1,0:T(8,128)} %get-tuple-element.28), channel_id=1, source_target_pairs={{0,1},{1,2},{2,3},{3,4},{4,5},{5,6},{6,7},{7,8},{8,9},{9,10},{10,1... | collective-permute-start | bytes 393224 | tf_op jit(solution)/shard_map/ppermute | solution.py:23
  32.6 4.1 copy-start.9
  36.6 10.2 %copy-start.1 = (f32[4,3,16,64,128]{4,3,2,0,1:T(8,128)}, f32[4,3,16,64,128]{4,3,2,0,1:T(8,128)S(1)}, u32[]{:S(2)}) copy-start(f32[4,3,16,64,128]{4,3,2,0,1:T(8,128)S(1)} %fusion.6) | copy-start | bytes 18874372
  36.7 11.5 %collective-permute-start.1 = (f32[5,64,128]{2,1,0:T(8,128)S(1)}, f32[5,64,128]{2,1,0:T(8,128)S(1)}, u32[]{:S(2)}, u32[]{:S(2)}) collective-permute-start(f32[5,64,128]{2,1,0:T(8,128)S(1)} %pad_maximum_fusion.6), channel_id=1, source_target_pairs={{0,1},{1,2},{2,3},{3,4},{4,5},{5,6},{6,7},{7,8},{8,9},{9,10},{10,1... | collective-permute-start | bytes 491528 | tf_op jit(solution)/shard_map/ppermute | solution.py:15
  207.8 25.3 %slice-start = ((s8[6291456]{0:T(1024)(128)(4,1)}), s8[4194304]{0:T(1024)(128)(4,1)S(1)}, s32[]{:S(2)}) async-start(s8[6291456]{0:T(1024)(128)(4,1)} %bitcast.104), calls=%async_computation.2 | async-start | bytes 8388608
  207.8 25.3 %slice-start.1 = ((s8[6291456]{0:T(1024)(128)(4,1)}), s8[2097152]{0:T(1024)(128)(4,1)S(1)}, s32[]{:S(2)}) async-start(s8[6291456]{0:T(1024)(128)(4,1)} %bitcast.104), calls=%async_computation.3 | async-start | bytes 4194304
  207.8 25.3 %copy-start.3 = (f32[4,16,64,128]{3,2,1,0:T(8,128)S(1)}, f32[4,16,64,128]{3,2,1,0:T(8,128)}, u32[]{:S(2)}) copy-start(f32[4,16,64,128]{3,2,1,0:T(8,128)} %get-tuple-element.19) | copy-start | bytes 6291460
  207.8 25.3 %copy-start.5 = (f32[4,16,64,128]{3,2,1,0:T(8,128)S(1)}, f32[4,16,64,128]{3,2,1,0:T(8,128)}, u32[]{:S(2)}) copy-start(f32[4,16,64,128]{3,2,1,0:T(8,128)} %get-tuple-element.20) | copy-start | bytes 6291460
  207.8 25.3 %copy-start.8 = (f32[16,64,128]{2,1,0:T(8,128)S(1)}, f32[16,64,128]{2,1,0:T(8,128)}, u32[]{:S(2)}) copy-start(f32[16,64,128]{2,1,0:T(8,128)} %get-tuple-element.34) | copy-start | bytes 1572868
  244.4 1.6 copy-start
  246.7 213.3 %collective-permute-start.3 = (f32[4,1,64,128]{3,2,1,0:T(8,128)}, f32[4,1,64,128]{3,2,1,0:T(8,128)S(1)}, u32[]{:S(2)}, u32[]{:S(2)}) collective-permute-start(f32[4,1,64,128]{3,2,1,0:T(8,128)} %get-tuple-element.25), channel_id=1, source_target_pairs={{1,0},{2,1},{3,2},{4,3},{5,4},{6,5},{7,6},{8,7},{9,8},{10,9},{11,1... | collective-permute-start | bytes 393224 | tf_op jit(solution)/shard_map/ppermute | solution.py:26
  249.3 210.7 %collective-permute-start.4 = (f32[4,1,64,128]{3,2,1,0:T(8,128)}, f32[4,1,64,128]{3,2,1,0:T(8,128)S(1)}, u32[]{:S(2)}, u32[]{:S(2)}) collective-permute-start(f32[4,1,64,128]{3,2,1,0:T(8,128)} %get-tuple-element.26), channel_id=1, source_target_pairs={{0,1},{1,2},{2,3},{3,4},{4,5},{5,6},{6,7},{7,8},{8,9},{9,10},{10,1... | collective-permute-start | bytes 393224 | tf_op jit(solution)/shard_map/ppermute | solution.py:23
  435.1 24.9 %slice-start.2 = ((s8[6291456]{0:T(1024)(128)(4,1)}), s8[4194304]{0:T(1024)(128)(4,1)S(1)}, s32[]{:S(2)}) async-start(s8[6291456]{0:T(1024)(128)(4,1)} %bitcast.106), calls=%async_computation.4 | async-start | bytes 8388608
  435.1 24.9 %slice-start.3 = ((s8[6291456]{0:T(1024)(128)(4,1)}), s8[2097152]{0:T(1024)(128)(4,1)S(1)}, s32[]{:S(2)}) async-start(s8[6291456]{0:T(1024)(128)(4,1)} %bitcast.106), calls=%async_computation.5 | async-start | bytes 4194304
  435.1 25.0 %copy-start.4 = (f32[4,16,64,128]{3,2,1,0:T(8,128)S(1)}, f32[4,16,64,128]{3,2,1,0:T(8,128)}, u32[]{:S(2)}) copy-start(f32[4,16,64,128]{3,2,1,0:T(8,128)} %get-tuple-element.19) | copy-start | bytes 6291460
  435.1 25.0 %copy-start.6 = (f32[4,16,64,128]{3,2,1,0:T(8,128)S(1)}, f32[4,16,64,128]{3,2,1,0:T(8,128)}, u32[]{:S(2)}) copy-start(f32[4,16,64,128]{3,2,1,0:T(8,128)} %get-tuple-element.20) | copy-start | bytes 6291460
  435.1 25.0 %copy-start.7 = (f32[4,15,64,128]{3,2,1,0:T(8,128)S(1)}, f32[4,15,64,128]{3,2,1,0:T(8,128)}, u32[]{:S(2)}) copy-start(f32[4,15,64,128]{3,2,1,0:T(8,128)} %slice_bitcast_fusion.2) | copy-start | bytes 5898244
Sparse Core Ops, SparseCore 0:
  9.7 176.0 all-gather.2
  244.5 168.3 all-gather.4
where the time goes:
time: 484 us; the launch traced here: 477 us
  waiting for transfers between devices  292 us (60%)
  local copies, waits for them, and re-layouts  64.5 us (13%)
  matrix products  50.2 us (10%)
  other arithmetic  41.5 us (9%)
  between operations  14.6 us (3%)
  starting transfers between devices  14.4 us (3%)
    all_gather x2, waiting for transfers between devices, coupled(): piece = lax.all_gather(field, 'inst', axis=0, tiled=True)  291 us
    dot_general x2, matrix products, coupled(): jnp.dot(dmat_rows, flat, precision=lax.Precision.HIGHEST, preferred_eleme...  50.2 us
    unnamed x36, local copies, waits for them, and re-layouts  46.5 us
    add x2, other arithmetic, lookup(): total = total + jnp.where(material == klass, table[klass], 0.0)  14.2 us
    sub x1, other arithmetic, body(): middle = field_start - relax_weight * residual / diag  11.2 us
    slice x4, local copies, waits for them, and re-layouts, next_along(): lax.slice_in_dim(field, 1, count, axis=axis)  10.7 us
    sub x1, other arithmetic, body(): field = middle - relax_weight * second / diag  9.77 us
  transfers between devices with their start and end apart: 7, of which 2 were waited for; matrix products, arithmetic and copies ran while one was open for 28% of the time, Pallas kernels for 0%

commit v1 on v0

--- a/solution.py
+++ b/solution.py
@@ -99,7 +99,8 @@
     dmat_rows = spectral_matrix(first, count)
 
     def coupled(field):
-        piece = lax.all_gather(field, "inst", axis=0, tiled=True)
+        stack = jnp.stack([field] * lax.axis_size("inst"))
+        piece = jnp.concatenate(lax.all_to_all(stack, "inst", 0, 0), axis=0)
         flat = piece.reshape(piece.shape[0], -1)
         product = jnp.dot(
             dmat_rows, flat, precision=lax.Precision.HIGHEST, preferred_element_type=jnp.float32

time: 484 us -> 659 us (1.36)
  the two profiles are of different devices: /device:TPU:1 before, /device:TPU:6 now
where the time goes in v1:
time: 659 us; the launch traced here: 652 us
  waiting for transfers between devices  453 us (69%)
  local copies, waits for them, and re-layouts  85.7 us (13%)
  matrix products  50.2 us (8%)
  other arithmetic  37.7 us (6%)
  starting transfers between devices  24.2 us (4%)
    all_to_all x2, waiting for transfers between devices, coupled(): piece = jnp.concatenate(lax.all_to_all(stack, 'inst', 0, 0), axis=0)  453 us
    dot_general x2, matrix products, coupled(): jnp.dot(dmat_rows, flat, precision=lax.Precision.HIGHEST, preferred_eleme...  50.2 us
    unnamed x32, local copies, waits for them, and re-layouts  28.2 us
    another operation x2, local copies, waits for them, and re-layouts, coupled(): flat = piece.reshape(piece.shape[0], -1)  24.2 us
    another operation x2, local copies, waits for them, and re-layouts, coupled(): stack = jnp.stack([field] * lax.axis_size('inst'))  17.4 us
  transfers between devices with their start and end apart: 7, of which 2 were waited for; matrix products, arithmetic and copies ran while one was open for 21% of the time, Pallas kernels for 0%

profile of v1, /device:TPU:6, one launch (start us, length us, event | category | flops | bytes accessed | tf_op | source)
XLA Modules:
  0.0 652.1 jit_solution(3142719800188936686)
XLA Ops:
  0.6 9.5 %stack.4 = f32[8,4,16,64,128]{4,3,2,1,0:T(8,128)} broadcast(f32[4,16,64,128]{3,2,1,0:T(8,128)} %param.6), dimensions={1,2,3,4} | broadcast | bytes 18874368 | tf_op jit(solution)/shard_map/stack | solution.py:102
  10.1 6.3 all-to-all-start
  17.0 5.6 select_add_fusion.1
  23.3 5.3 select_add_fusion
  28.9 4.0 fusion.6
  35.8 4.7 collective-permute-start.2
  40.5 2.4 slice_bitcast_fusion.1
  42.9 2.3 fusion.81
  45.2 2.7 fusion.82
  51.4 215.1 %all-to-all-done = f32[8,4,16,64,128]{4,3,2,1,0:T(8,128)} async-done(((f32[8,4,16,64,128]{4,3,2,1,0:T(8,128)}), f32[8,4,16,64,128]{4,3,2,1,0:T(8,128)}, u32[]{:S(2)}, u32[]{:S(2)}) %all-to-all-start) | async-done | bytes 16777248 | tf_op jit(solution)/shard_map/all_to_all | solution.py:103
  266.4 12.1 %reshape_reshape.6 = f32[32,131072]{1,0:T(8,128)} reshape(f32[8,4,16,64,128]{4,3,2,1,0:T(8,128)} %all-to-all-done) | data formatting | bytes 33554432 | tf_op jit(solution)/shard_map/reshape;reshape | solution.py:104
  278.5 14.1 %copy.106 = f32[4,8,1024,128]{3,2,1,0:T(8,128)} copy(f32[4,8,1024,128]{3,1,2,0:T(8,128)} %bitcast.99) | data formatting | bytes 33554432
  292.6 25.3 %fusion.2 = f32[4,16,64,128]{3,0,2,1:T(4,128)} fusion(f32[16,64,128,32]{2,1,0,3:T(8,128)} %bitcast.100, s32[4]{0:T(128)S(1)} %iota_add_fusion), kind=kOutput, calls=%fused_computation.2 | convolution fusion | flops 201329536 | bytes 18874384 | tf_op jit(solution)/shard_map/dot_general | solution.py:105
  318.0 10.7 %divide_subtract_fusion = (f32[4,16,64,128]{3,2,1,0:T(8,128)S(1)}, f32[4,16,64,128]{3,2,1,0:T(8,128)}) fusion(f32[4,16,64,128]{3,2,1,0:T(8,128)S(1)} %copy-done.2, f32[4,16,64,127]{3,2,1,0:T(8,128)} %bitcast.106, f32[4,16,63,128]{3,2,1,0:T(8,128)S(1)} %bitcast.104, f32[4,3,16,64,128]{4,3,2,0,1:T(8,128)S(1)} %bitcast.95, ...), kind=kLoop, calls=%fused_computation.59 | loop fusion | flops 38273024 | bytes 35241984 | tf_op jit(solution)/shard_map/sub | solution.py:136
  328.6 7.9 %stack.5 = f32[8,4,16,64,128]{4,3,2,1,0:T(8,128)} broadcast(f32[4,16,64,128]{3,2,1,0:T(8,128)S(1)} %get-tuple-element.6), dimensions={1,2,3,4} | broadcast | bytes 18874368 | tf_op jit(solution)/shard_map/stack | solution.py:102
  336.5 6.2 all-to-all-start.1
  344.7 3.0 collective-permute-start.4
  347.8 2.3 fusion.77
  350.1 2.7 fusion.78
  352.8 238.1 %all-to-all-done.1 = f32[8,4,16,64,128]{4,3,2,1,0:T(8,128)} async-done(((f32[8,4,16,64,128]{4,3,2,1,0:T(8,128)}), f32[8,4,16,64,128]{4,3,2,1,0:T(8,128)}, u32[]{:S(2)}, u32[]{:S(2)}) %all-to-all-start.1) | async-done | bytes 16777248 | tf_op jit(solution)/shard_map/all_to_all | solution.py:103
  591.0 12.1 %reshape_reshape.7 = f32[32,131072]{1,0:T(8,128)} reshape(f32[8,4,16,64,128]{4,3,2,1,0:T(8,128)} %all-to-all-done.1) | data formatting | bytes 33554432 | tf_op jit(solution)/shard_map/reshape;reshape | solution.py:104
  603.1 14.1 %copy.107 = f32[4,8,1024,128]{3,2,1,0:T(8,128)} copy(f32[4,8,1024,128]{3,1,2,0:T(8,128)} %bitcast.101) | data formatting | bytes 33554432
  617.2 24.9 %fusion = f32[4,16,64,128]{3,0,2,1:T(4,128)} fusion(f32[16,64,128,32]{2,1,0,3:T(8,128)} %bitcast.98, s32[4]{0:T(128)S(1)} %iota_add_fusion), kind=kOutput, calls=%fused_computation | convolution fusion | flops 201329536 | bytes 18874384 | tf_op jit(solution)/shard_map/dot_general | solution.py:105
  642.1 9.8 %fusion.18 = f32[4,16,64,128]{3,2,1,0:T(8,128)} fusion(f32[4,16,64,128]{3,2,1,0:T(8,128)S(1)} %get-tuple-element.6, f32[4,16,64,128]{3,2,1,0:T(8,128)} %param.7, f32[4,1,64,128]{3,2,1,0:T(8,128)S(1)} %collective-permute-done.4, f32[4,1,64,128]{3,2,1,0:T(8,128)S(1)} %collective-permute-done.3, f32[4,16,64,128]{3,0,2,1:T(4,128)} %fusion, ...), kind=kLoop, calls=%fused_computation.20 | loop fusion | flops 38273024 | bytes 33144832 | tf_op jit(solution)/shard_map/sub | solution.py:138
  (55 shorter events, 9.7 us)
Async XLA Ops:
  10.1 6.3 copy-start.9
  10.1 6.9 %copy-start.8 = (s32[16,64,128]{2,1,0:T(8,128)S(1)}, s32[16,64,128]{2,1,0:T(8,128)}, u32[]{:S(2)}) copy-start(s32[16,64,128]{2,1,0:T(8,128)} %param.8) | copy-start | bytes 1572868
  10.1 256.3 %all-to-all-start = ((f32[8,4,16,64,128]{4,3,2,1,0:T(8,128)}), f32[8,4,16,64,128]{4,3,2,1,0:T(8,128)}, u32[]{:S(2)}, u32[]{:S(2)}) async-start(f32[8,4,16,64,128]{4,3,2,1,0:T(8,128)} %stack.4), calls=%async_computation | async-start | bytes 33554432 | tf_op jit(solution)/shard_map/all_to_all | solution.py:103
  16.4 6.3 copy-start.10
  28.9 5.5 copy-start.1
  33.0 15.0 %copy-start = (f32[4,3,16,64,128]{4,3,2,0,1:T(8,128)}, f32[4,3,16,64,128]{4,3,2,0,1:T(8,128)S(1)}, u32[]{:S(2)}) copy-start(f32[4,3,16,64,128]{4,3,2,0,1:T(8,128)S(1)} %fusion.6) | copy-start | bytes 18874372
  33.0 16.4 %collective-permute-start.1 = (f32[5,64,128]{2,1,0:T(8,128)S(1)}, f32[5,64,128]{2,1,0:T(8,128)S(1)}, u32[]{:S(2)}, u32[]{:S(2)}) collective-permute-start(f32[5,64,128]{2,1,0:T(8,128)S(1)} %pad_maximum_fusion.6), channel_id=1, source_target_pairs={{0,1},{1,2},{2,3},{3,4},{4,5},{5,6},{6,7},{7,8},{8,9},{9,10},{10,1... | collective-permute-start | bytes 491528 | tf_op jit(solution)/shard_map/ppermute | solution.py:15
  34.5 283.4 %collective-permute-start = (f32[4,1,64,128]{3,2,1,0:T(8,128)S(1)}, f32[4,1,64,128]{3,2,1,0:T(8,128)S(1)}, u32[]{:S(2)}, u32[]{:S(2)}) collective-permute-start(f32[4,1,64,128]{3,2,1,0:T(8,128)S(1)} %get-tuple-element.25), channel_id=1, source_target_pairs={{1,0},{2,1},{3,2},{4,3},{5,4},{6,5},{7,6},{8,7},{9,8},{10,9},{11,1... | collective-permute-start | bytes 393224 | tf_op jit(solution)/shard_map/ppermute | solution.py:26
  35.8 282.1 %collective-permute-start.2 = (f32[4,1,64,128]{3,2,1,0:T(8,128)S(1)}, f32[4,1,64,128]{3,2,1,0:T(8,128)S(1)}, u32[]{:S(2)}, u32[]{:S(2)}) collective-permute-start(f32[4,1,64,128]{3,2,1,0:T(8,128)S(1)} %get-tuple-element.26), channel_id=1, source_target_pairs={{0,1},{1,2},{2,3},{3,4},{4,5},{5,6},{6,7},{7,8},{8,9},{9,10},{10,1... | collective-permute-start | bytes 393224 | tf_op jit(solution)/shard_map/ppermute | solution.py:23
  292.6 25.3 %slice-start = ((s8[6291456]{0:T(1024)(128)(4,1)}), s8[4194304]{0:T(1024)(128)(4,1)S(1)}, s32[]{:S(2)}) async-start(s8[6291456]{0:T(1024)(128)(4,1)} %bitcast.94), calls=%async_computation.2 | async-start | bytes 8388608
  292.6 25.3 %slice-start.1 = ((s8[6291456]{0:T(1024)(128)(4,1)}), s8[2097152]{0:T(1024)(128)(4,1)S(1)}, s32[]{:S(2)}) async-start(s8[6291456]{0:T(1024)(128)(4,1)} %bitcast.94), calls=%async_computation.3 | async-start | bytes 4194304
  292.6 25.3 %copy-start.2 = (f32[4,16,64,128]{3,2,1,0:T(8,128)S(1)}, f32[4,16,64,128]{3,2,1,0:T(8,128)}, u32[]{:S(2)}) copy-start(f32[4,16,64,128]{3,2,1,0:T(8,128)} %param.6) | copy-start | bytes 6291460
  292.6 25.3 %copy-start.3 = (f32[4,16,64,128]{3,2,1,0:T(8,128)S(1)}, f32[4,16,64,128]{3,2,1,0:T(8,128)}, u32[]{:S(2)}) copy-start(f32[4,16,64,128]{3,2,1,0:T(8,128)} %get-tuple-element.17) | copy-start | bytes 6291460
  292.6 25.3 %copy-start.7 = (f32[16,64,128]{2,1,0:T(8,128)S(1)}, f32[16,64,128]{2,1,0:T(8,128)}, u32[]{:S(2)}) copy-start(f32[16,64,128]{2,1,0:T(8,128)} %get-tuple-element.32) | copy-start | bytes 1572868
  336.5 254.5 %all-to-all-start.1 = ((f32[8,4,16,64,128]{4,3,2,1,0:T(8,128)}), f32[8,4,16,64,128]{4,3,2,1,0:T(8,128)}, u32[]{:S(2)}, u32[]{:S(2)}) async-start(f32[8,4,16,64,128]{4,3,2,1,0:T(8,128)} %stack.5), calls=%async_computation.1 | async-start | bytes 33554432 | tf_op jit(solution)/shard_map/all_to_all | solution.py:103
  343.4 298.6 %collective-permute-start.3 = (f32[4,1,64,128]{3,2,1,0:T(8,128)}, f32[4,1,64,128]{3,2,1,0:T(8,128)S(1)}, u32[]{:S(2)}, u32[]{:S(2)}) collective-permute-start(f32[4,1,64,128]{3,2,1,0:T(8,128)} %get-tuple-element.23), channel_id=1, source_target_pairs={{1,0},{2,1},{3,2},{4,3},{5,4},{6,5},{7,6},{8,7},{9,8},{10,9},{11,1... | collective-permute-start | bytes 393224 | tf_op jit(solution)/shard_map/ppermute | solution.py:26
  344.7 297.4 %collective-permute-start.4 = (f32[4,1,64,128]{3,2,1,0:T(8,128)}, f32[4,1,64,128]{3,2,1,0:T(8,128)S(1)}, u32[]{:S(2)}, u32[]{:S(2)}) collective-permute-start(f32[4,1,64,128]{3,2,1,0:T(8,128)} %get-tuple-element.24), channel_id=1, source_target_pairs={{0,1},{1,2},{2,3},{3,4},{4,5},{5,6},{6,7},{7,8},{8,9},{9,10},{10,1... | collective-permute-start | bytes 393224 | tf_op jit(solution)/shard_map/ppermute | solution.py:23
  617.1 24.9 %slice-start.2 = ((s8[6291456]{0:T(1024)(128)(4,1)}), s8[4194304]{0:T(1024)(128)(4,1)S(1)}, s32[]{:S(2)}) async-start(s8[6291456]{0:T(1024)(128)(4,1)} %bitcast.96), calls=%async_computation.4 | async-start | bytes 8388608
  617.1 25.0 %slice-start.3 = ((s8[6291456]{0:T(1024)(128)(4,1)}), s8[2097152]{0:T(1024)(128)(4,1)S(1)}, s32[]{:S(2)}) async-start(s8[6291456]{0:T(1024)(128)(4,1)} %bitcast.96), calls=%async_computation.5 | async-start | bytes 4194304
  617.1 25.0 %copy-start.4 = (f32[4,16,64,128]{3,2,1,0:T(8,128)S(1)}, f32[4,16,64,128]{3,2,1,0:T(8,128)}, u32[]{:S(2)}) copy-start(f32[4,16,64,128]{3,2,1,0:T(8,128)} %get-tuple-element.17) | copy-start | bytes 6291460
  617.1 25.0 %copy-start.5 = (f32[4,16,64,128]{3,2,1,0:T(8,128)S(1)}, f32[4,16,64,128]{3,2,1,0:T(8,128)}, u32[]{:S(2)}) copy-start(f32[4,16,64,128]{3,2,1,0:T(8,128)} %get-tuple-element.18) | copy-start | bytes 6291460
  617.1 25.0 %copy-start.6 = (f32[4,15,64,128]{3,2,1,0:T(8,128)S(1)}, f32[4,15,64,128]{3,2,1,0:T(8,128)}, u32[]{:S(2)}) copy-start(f32[4,15,64,128]{3,2,1,0:T(8,128)} %slice_bitcast_fusion.2) | copy-start | bytes 5898244
